TPU v7x, 256 devices: a whole 4x4x8 slice. The times are simulated.
256 devices in a mesh: seq: 32 (over x, y, core), dp: 8 (over z).
Axes of the slice: x: 4, y: 4, z: 8, core: 2. Of those that a mesh axis runs over, the one named last changes fastest.
Arguments:
- queries: bfloat16 [8, 16384, 2048], P('dp', 'seq'), may hold values from -5 to 5
- keys: bfloat16 [8, 16384, 2048], P('dp', 'seq'), may hold values from -5 to 5
- values: bfloat16 [8, 16384, 2048], P('dp', 'seq'), may hold values from -8 to 8
- out_weight: bfloat16 [2048, 4096], P(None, 'dp'), may hold values from -0.125 to 0.125
Outputs:
- projected: bfloat16 [8, 16384, 4096], P('dp', 'seq')
All inputs are finite; a program needn't handle non-finite values.
Results may differ from a plain program's by a relative error of at most 0.0061.
Values may be sent and summed in bfloat16 or wider, within the bound.
No kernel may reach another device: no remote copies, remote signals or barrier semaphores. Data moves between devices by JAX's collectives and lax.ppermute only.
A program may use at most 192 MiB of HBM per device.

v0:
```python
import math
import jax
import jax.numpy as jnp
from jax import lax
from jax.sharding import PartitionSpec as P

CHANNEL_WIDTH = 128
SEGMENT_LENGTH = 256


def prefix(value, axis, join, neutral):
    count, mine = (lax.axis_size(axis), lax.axis_index(axis))
    pieces = jax.tree.map(lambda part: lax.all_gather(part, axis), value)
    subtotal = jax.tree.map(
        lambda part, zero: jnp.full_like(part, 0) + jnp.asarray(zero, part.dtype), value, neutral
    )

    def turn(position, subtotal):
        longer = join(subtotal, jax.tree.map(lambda part: part[position], pieces))
        return jax.tree.map(lambda new, old: jnp.where(position < mine, new, old), longer, subtotal)

    return lax.fori_loop(0, count - 1, turn, subtotal)


def shifted(block, axis, distance):
    devices = range(lax.axis_size(axis))
    route = [(i - distance, i) for i in devices if i - distance in devices]
    return lax.ppermute(block, axis, route)


def add_pair(earlier_pair, later_pair):
    return (earlier_pair[0] + later_pair[0], earlier_pair[1] + later_pair[1])


def per_device(queries, keys, values, out_weight):
    local_rows = queries.shape[1]
    feature_width = queries.shape[2]
    head_count = feature_width // CHANNEL_WIDTH
    local_blocks = local_rows // SEGMENT_LENGTH
    shard_count = lax.axis_size("seq")
    shard_index = lax.axis_index("seq")
    total_blocks = local_blocks * shard_count
    first_block = shard_index * local_blocks
    softmax_multiplier = 1.0 / math.sqrt(CHANNEL_WIDTH)
    faraway_offset_bias = math.log(SEGMENT_LENGTH)
    own_queries = queries[0]
    own_keys = keys[0]
    own_values = values[0]
    span_address_means = jnp.mean(
        own_keys.reshape(local_blocks, SEGMENT_LENGTH, feature_width), axis=1, dtype=jnp.float32
    ).astype(jnp.bfloat16)
    value_means = jnp.mean(
        own_values.reshape(local_blocks, SEGMENT_LENGTH, feature_width), axis=1, dtype=jnp.float32
    ).astype(jnp.bfloat16)
    empty_buffer = jnp.zeros((total_blocks, feature_width), jnp.bfloat16)
    slot_keys = lax.dynamic_update_slice_in_dim(empty_buffer, span_address_means, first_block, 0)
    slot_values = lax.dynamic_update_slice_in_dim(empty_buffer, value_means, first_block, 0)
    far_keys, far_values = prefix(
        (slot_keys, slot_values), "seq", add_pair, (empty_buffer, empty_buffer)
    )
    prev_keys, prev_values = shifted(
        (own_keys[local_rows - SEGMENT_LENGTH :], own_values[local_rows - SEGMENT_LENGTH :]),
        "seq",
        1,
    )
    near_keys = jnp.concatenate([prev_keys, own_keys], axis=0)
    near_values = jnp.concatenate([prev_values, own_values], axis=0)
    far_k = far_keys.reshape(total_blocks, head_count, CHANNEL_WIDTH)
    far_v = far_values.reshape(total_blocks, head_count, CHANNEL_WIDTH)
    far_index = jnp.arange(total_blocks, dtype=jnp.int32)
    group_rows = SEGMENT_LENGTH * math.gcd(local_blocks, max(1, 512 // SEGMENT_LENGTH))
    request_vectors = own_queries.reshape(group_rows, head_count, CHANNEL_WIDTH)
    address_vectors = near_keys.reshape(group_rows + SEGMENT_LENGTH, head_count, CHANNEL_WIDTH)
    value_rows = near_values.reshape(group_rows + SEGMENT_LENGTH, head_count, CHANNEL_WIDTH)
    query_local = 0 + jnp.arange(group_rows, dtype=jnp.int32)
    key_local = 0 - SEGMENT_LENGTH + jnp.arange(group_rows + SEGMENT_LENGTH, dtype=jnp.int32)
    query_blk = query_local // SEGMENT_LENGTH
    key_blk = key_local // SEGMENT_LENGTH
    within_block = (key_blk[None, :] == query_blk[:, None]) & (
        key_local[None, :] <= query_local[:, None]
    )
    preceding_segment = (key_blk[None, :] == query_blk[:, None] - 1) & (
        (key_blk[None, :] >= 0) | (shard_index > 0)
    )
    adjacent_similarity = (
        jnp.einsum(
            "qhd,khd->hqk", request_vectors, address_vectors, preferred_element_type=jnp.float32
        )
        * softmax_multiplier
    )
    adjacent_similarity = jnp.where(
        (within_block | preceding_segment)[None], adjacent_similarity, -jnp.inf
    )
    query_global = first_block + query_blk
    faraway_similarity = (
        jnp.einsum("qhd,jhd->hqj", request_vectors, far_k, preferred_element_type=jnp.float32)
        * softmax_multiplier
        + faraway_offset_bias
    )
    faraway_similarity = jnp.where(
        (far_index[None, :] < query_global[:, None] - 1)[None], faraway_similarity, -jnp.inf
    )
    row_max = jnp.maximum(
        jnp.max(adjacent_similarity, axis=-1), jnp.max(faraway_similarity, axis=-1)
    )[..., None]
    near_w = jnp.exp(adjacent_similarity - row_max)
    far_w = jnp.exp(faraway_similarity - row_max)
    row_total = jnp.sum(near_w, axis=-1, keepdims=True) + jnp.sum(far_w, axis=-1, keepdims=True)
    near_p = (near_w / row_total).astype(jnp.bfloat16)
    far_p = (far_w / row_total).astype(jnp.bfloat16)
    attended = jnp.einsum("hqk,khd->qhd", near_p, value_rows, preferred_element_type=jnp.float32)
    attended = attended + jnp.einsum(
        "hqj,jhd->qhd", far_p, far_v, preferred_element_type=jnp.float32
    )
    pieces = attended.astype(jnp.bfloat16).reshape(group_rows, feature_width)
    projected = jnp.dot(
        pieces,
        lax.all_gather(out_weight, "dp", axis=1, tiled=True),
        preferred_element_type=jnp.float32,
    ).astype(jnp.bfloat16)
    return projected[None]


def solution(mesh):
    return jax.shard_map(
        per_device,
        mesh=mesh,
        in_specs=(P("dp", "seq", None), P("dp", "seq", None), P("dp", "seq", None), P(None, "dp")),
        out_specs=P("dp", "seq", None),
        check_vma=False,
    )
```

profile of v0, /device:TPU:1, one launch (start us, length us, event | category | flops | bytes accessed | tf_op | source)
XLA Modules:
  0.0 340.8 jit_solution(379502660158891560)
XLA Ops:
  6.5 2.1 convert_reduce_fusion.1
  8.7 0.7 copy-done.5
  9.4 0.0 all-gather.4.cloned.1.call-update
  9.5 0.0 all-gather.6.cloned.1.call-start
  9.5 0.4 convert_reduce_fusion
  10.0 0.7 copy-done.4
  10.7 0.0 all-gather.6.cloned.1.call-update
  10.7 0.0 all-gather.8.cloned.1.call-start
  10.8 0.7 all-gather.8.cloned.1.call-update
  11.4 3.9 %copy.25 = bf16[1,512,2048]{1,2,0:T(8,128)(2,1)} copy(bf16[1,512,2048]{2,1,0:T(8,128)(2,1)} %param.7) | data formatting | bytes 4194304 | tf_op args[1]
  15.4 2.3 slice_bitcast_fusion
  17.7 4.6 %collective-permute-start.1 = (bf16[256,2048]{0,1:T(8,128)(2,1)}, bf16[256,2048]{0,1:T(8,128)(2,1)}, u32[]{:S(2)}, u32[]{:S(2)}) collective-permute-start(bf16[256,2048]{0,1:T(8,128)(2,1)} %slice_bitcast_fusion), channel_id=1, source_target_pairs={{0,8},{8,16},{16,24},{24,32},{32,40},{40,48},{48,56},{56,64},{64,7... | collective-permute-start | bytes 3145736 | tf_op jit(solution)/shard_map/ppermute | solution.py:28
  22.2 1.0 slice_bitcast_fusion.1
  23.3 1.9 collective-permute-start
  25.2 2.5 copy.24
  27.7 3.7 %copy.37 = bf16[64,8,16,128]{3,2,1,0:T(8,128)(2,1)} copy(bf16[64,8,16,128]{3,1,2,0:T(8,128)(2,1)} %bitcast.68) | data formatting | bytes 4194304
  31.4 2.4 copy.28
  33.9 0.8 fusion.20
  34.7 3.3 collective-permute-done.1
  38.1 2.3 copy.27
  40.3 9.4 %collective-permute-done = bf16[256,2048]{1,0:T(8,128)(2,1)} collective-permute-done((bf16[256,2048]{1,0:T(8,128)(2,1)}, bf16[256,2048]{1,0:T(8,128)(2,1)}, u32[]{:S(2)}, u32[]{:S(2)}) %collective-permute-start) | collective-permute-done | bytes 1048608 | tf_op jit(solution)/shard_map/ppermute | solution.py:28
  49.7 2.3 copy.23
  52.0 12.3 %fusion.1 = (f32[16,512]{1,0:T(8,128)S(1)}, f32[16,768,512]{2,1,0:T(8,128)}) fusion(pred[512,768]{0,1:T(8,128)(4,1)S(1)} %fusion.20, bf16[512,16,128]{2,1,0:T(8,128)(2,1)S(1)} %bitcast.70, bf16[512,16,128]{2,0,1:T(8,128)(2,1)} %copy.28, bf16[256,16,128]{2,0,1:T(8,128)(2,1)} %copy.27), kind=kOutput, calls=%fused_computation.6 | convolution fusion | flops 1635770368 | bytes 30834688 | tf_op jit(solution)/shard_map/qhd,khd->hqk/dot_general | solution.py:86
  64.3 21.8 %all-gather.4.cloned.1.call-done = bf16[32,64,2048]{2,1,0:T(8,128)(2,1)} async-done(((bf16[1,64,2048]{2,1,0:T(8,128)(2,1)}), bf16[32,64,2048]{2,1,0:T(8,128)(2,1)}) %all-gather.4.cloned.1.call-update) | async-done | bytes 8388624 | tf_op jit(solution)/shard_map/all_gather | solution.py:13
  86.1 60.0 %all-gather.6.cloned.1.call-done = bf16[32,64,2048]{2,1,0:T(8,128)(2,1)} async-done(((bf16[1,64,2048]{2,1,0:T(8,128)(2,1)}), bf16[32,64,2048]{2,1,0:T(8,128)(2,1)}) %all-gather.6.cloned.1.call-update) | async-done | bytes 8388624 | tf_op jit(solution)/shard_map/all_gather | solution.py:13
  146.2 39.2 %while.16 = (s32[]{:T(128)}, bf16[64,2048]{1,0:T(8,128)(2,1)S(1)}, bf16[64,2048]{1,0:T(8,128)(2,1)S(1)}, s32[]{:T(128)}, bf16[32,64,2048]{2,1,0:T(8,128)(2,1)}, ...) while((s32[]{:T(128)}, bf16[64,2048]{1,0:T(8,128)(2,1)S(1)}, ...), condition=%wide.region_4.5_spmd.clone, body=%wide.region_3.4_spmd.clone.sunk | while | flops 786436 | bytes 1572973 | solution.py:22
  146.2 1.2 add_select_fusion.5
  147.4 1.2 add_select_fusion.5
  148.7 1.2 add_select_fusion.5
  149.9 1.2 add_select_fusion.5
  151.2 1.2 add_select_fusion.5
  152.5 1.2 add_select_fusion.5
  153.7 1.2 add_select_fusion.5
  155.0 1.2 add_select_fusion.5
  156.2 1.2 add_select_fusion.5
  157.5 1.2 add_select_fusion.5
  158.8 1.3 add_select_fusion.5
  160.1 1.3 add_select_fusion.5
  161.4 1.2 add_select_fusion.5
  162.6 1.2 add_select_fusion.5
  163.9 1.2 add_select_fusion.5
  165.2 1.2 add_select_fusion.5
  166.4 1.2 add_select_fusion.5
  167.7 1.2 add_select_fusion.5
  168.9 1.2 add_select_fusion.5
  170.2 1.2 add_select_fusion.5
  171.5 1.2 add_select_fusion.5
  172.7 1.2 add_select_fusion.5
  174.0 1.2 add_select_fusion.5
  175.3 1.2 add_select_fusion.5
  176.5 1.2 add_select_fusion.5
  177.8 1.2 add_select_fusion.5
  179.1 1.2 add_select_fusion.5
  180.3 1.2 add_select_fusion.5
  181.6 1.2 add_select_fusion.5
  182.9 1.2 add_select_fusion.5
  184.1 1.2 add_select_fusion.5
  185.4 1.5 fusion.42
  186.9 0.4 fusion.11
  187.3 11.3 %fusion = f32[16,512]{1,0:T(8,128)S(1)} fusion(f32[16,768,512]{2,1,0:T(8,128)} %get-tuple-element.153, f32[16,512]{1,0:T(8,128)S(1)} %max.7, pred[512,768]{0,1:T(8,128)(4,1)S(1)} %fusion.20), kind=kLoop, calls=%fused_computation.5 | loop fusion | flops 25157632 | bytes 25624576 | tf_op jit(solution)/shard_map/reduce_sum | solution.py:108
  198.5 2.8 fusion.21
  201.3 14.6 %add_convert_fusion = bf16[16,128,512]{2,1,0:T(8,128)(2,1)} fusion(f32[16,128,512]{2,1,0:T(8,128)} %fusion.21, f32[16,768,512]{2,1,0:T(8,128)} %get-tuple-element.153, f32[16,512]{1,0:T(8,128)S(1)} %add.130, f32[16,512]{1,0:T(8,128)S(1)} %max.7, pred[512,768]{0,1:T(8,128)(4,1)S(1)} %fusion.20, bf16[512,16,128]{0,2,1:T(8,128)(2,1)S(1)} %bitcast.69, ...), kind=kOutput, calls=%fused_computation.12 | convolution fusion | flops 1650458624 | bytes 35061760 | tf_op jit(solution)/shard_map/hqk,khd->qhd/dot_general | solution.py:111
  215.9 103.9 %all-gather.8.cloned.1.call-done = bf16[2048,4096]{1,0:T(8,128)(2,1)} async-done(((bf16[2048,512]{1,0:T(8,128)(2,1)}), bf16[2048,4096]{1,0:T(8,128)(2,1)}) %all-gather.8.cloned.1.call-update) | async-done | bytes 16777232 | tf_op jit(solution)/shard_map/all_gather | solution.py:118
  319.8 14.5 %fusion.3 = bf16[1,512,4096]{2,1,0:T(8,128)(2,1)} fusion(bf16[512,2048]{0,1:T(8,128)(2,1)} %bitcast.73, bf16[2048,4096]{1,0:T(8,128)(2,1)} %all-gather.8.cloned.1.call-done), kind=kOutput, calls=%fused_computation.9 | convolution fusion | flops 8592031744 | bytes 23068672 | tf_op jit(solution)/shard_map/dot_general | solution.py:116
  (24 shorter events, 0.2 us)
Async XLA Ops:
  6.5 3.0 copy-start
  6.5 79.6 %all-gather.4.cloned.1.call-start = ((), (), s32[]{:S(2)}) async-start(), calls=%async_computation | async-start | bytes 8650752 | tf_op jit(solution)/shard_map/all_gather | solution.py:13
  8.7 0.7 copy-start.5
  9.5 136.7 %all-gather.6.cloned.1.call-start = ((), (), s32[]{:S(2)}) async-start(), calls=%async_computation.1 | async-start | bytes 8650752 | tf_op jit(solution)/shard_map/all_gather | solution.py:13
  10.0 0.7 copy-start.4
  10.7 309.1 %all-gather.8.cloned.1.call-start = ((), (), s32[]{:S(2)}) async-start(), calls=%async_computation.2 | async-start | bytes 18874368 | tf_op jit(solution)/shard_map/all_gather | solution.py:118
  17.7 20.4 %collective-permute-start.1 = (bf16[256,2048]{0,1:T(8,128)(2,1)}, bf16[256,2048]{0,1:T(8,128)(2,1)}, u32[]{:S(2)}, u32[]{:S(2)}) collective-permute-start(bf16[256,2048]{0,1:T(8,128)(2,1)} %slice_bitcast_fusion), channel_id=1, source_target_pairs={{0,8},{8,16},{16,24},{24,32},{32,40},{40,48},{48,56},{56,64},{64,7... | collective-permute-start | bytes 3145736 | tf_op jit(solution)/shard_map/ppermute | solution.py:28
  23.3 26.4 %collective-permute-start = (bf16[256,2048]{1,0:T(8,128)(2,1)}, bf16[256,2048]{1,0:T(8,128)(2,1)}, u32[]{:S(2)}, u32[]{:S(2)}) collective-permute-start(bf16[256,2048]{1,0:T(8,128)(2,1)} %slice_bitcast_fusion.1), channel_id=1, source_target_pairs={{0,8},{8,16},{16,24},{24,32},{32,40},{40,48},{48,56},{56,64},{64,7... | collective-permute-start | bytes 3145736 | tf_op jit(solution)/shard_map/ppermute | solution.py:28
  27.7 3.7 %copy-start.1 = (bf16[1,512,2048]{1,2,0:T(8,128)(2,1)S(1)}, bf16[1,512,2048]{1,2,0:T(8,128)(2,1)}, u32[]{:S(2)}) copy-start(bf16[1,512,2048]{1,2,0:T(8,128)(2,1)} %copy.25) | copy-start | bytes 6291460
  33.8 18.2 %copy-start.3 = (bf16[64,8,16,128]{3,2,1,0:T(8,128)(2,1)S(1)}, bf16[64,8,16,128]{3,2,1,0:T(8,128)(2,1)}, u32[]{:S(2)}) copy-start(bf16[64,8,16,128]{3,2,1,0:T(8,128)(2,1)} %copy.37) | copy-start | bytes 6291460
  198.5 2.8 copy-start.2
Sparse Core Ops, SparseCore 0:
  9.9 76.2 all-gather.3
  88.7 57.4 all-gather.5
  148.0 171.7 all-gather.7
where the time goes:
time: 342 us; the launch traced here: 341 us
  waiting for transfers between devices  199 us (58%)
  other arithmetic  53.6 us (16%)
  matrix products  45.6 us (13%)
  local copies, waits for them, and re-layouts  21.8 us (6%)
  between operations  13.3 us (4%)
  starting transfers between devices  6.57 us (2%)
    all_gather x1, waiting for transfers between devices, per_device(): lax.all_gather(out_weight, 'dp', axis=1, tiled=True)  104 us
    all_gather x2, waiting for transfers between devices, prefix(): pieces = jax.tree.map(lambda part: lax.all_gather(part, axis), value)  81.8 us
    select_n x31, other arithmetic, turn(): jnp.where(position < mine, new, old)  38.5 us
    dot_general x1, matrix products, per_device(): jnp.einsum('hqk,khd->qhd', near_p, value_rows, preferred_element_type=jnp...  14.6 us
    dot_general x1, matrix products, per_device(): jnp.dot(pieces, lax.all_gather(out_weight, 'dp', axis=1, tiled=True), pre...  14.5 us
    ppermute x2, waiting for transfers between devices, shifted(): return lax.ppermute(block, axis, route)  12.7 us
    dot_general x1, matrix products, per_device(): jnp.einsum('qhd,khd->hqk', request_vectors, address_vectors, preferred_el...  12.3 us
    unnamed x15, local copies, waits for them, and re-layouts  11.5 us
  transfers between devices with their start and end apart: 5, of which 5 were waited for; matrix products, arithmetic and copies ran while one was open for 30% of the time, Pallas kernels for 0%

commit v1 on v0

--- a/solution.py
+++ b/solution.py
@@ -1,3 +1,4 @@
+import functools
 import math
 import jax
 import jax.numpy as jnp
@@ -6,6 +7,17 @@
 
 CHANNEL_WIDTH = 128
 SEGMENT_LENGTH = 256
+
+
+def _show_ways(frame_in, device_axis):
+    in_order = []
+    for _ in range(lax.axis_size(device_axis)):
+        in_order.append(frame_in)
+    u_next = lax.all_to_all(jnp.concatenate(in_order, 1), device_axis, 1, 1, tiled=True)
+    return u_next
+
+
+sections_change = functools.partial(_show_ways, device_axis="dp")
 
 
 def prefix(value, axis, join, neutral):
@@ -114,9 +126,7 @@
     )
     pieces = attended.astype(jnp.bfloat16).reshape(group_rows, feature_width)
     projected = jnp.dot(
-        pieces,
-        lax.all_gather(out_weight, "dp", axis=1, tiled=True),
-        preferred_element_type=jnp.float32,
+        pieces, sections_change(out_weight), preferred_element_type=jnp.float32
     ).astype(jnp.bfloat16)
     return projected[None]
 

time: 342 us -> 464 us (1.36)
  waiting for transfers between devices: 199 us -> 258 us
  local copies, waits for them, and re-layouts: 21.8 us -> 75.1 us
  starting transfers between devices: 6.57 us -> 15.2 us
    all_to_all x0 -> x1, waiting for transfers between devices: none -> 217 us  [_show_ways(): lax.all_to_all(jnp.concatenate(in_order, 1), device_axis, 1, 1, tiled=True)]
    all_gather x1 -> x0, waiting for transfers between devices: 104 us -> none  [per_device(): lax.all_gather(out_weight, 'dp', axis=1, tiled=True)]
    all_gather x2, waiting for transfers between devices: 81.8 us -> 28.5 us  [prefix(): pieces = jax.tree.map(lambda part: lax.all_gather(part, axis), value)]
    all_to_all x0 -> x2, local copies, waits for them, and re-layouts: none -> 43.2 us  [_show_ways(): lax.all_to_all(jnp.concatenate(in_order, 1), device_axis, 1, 1, tiled=True)]
    unnamed x15 -> x27, local copies, waits for them, and re-layouts: 11.5 us -> 21.4 us
    all_to_all x0 -> x1, starting transfers between devices: none -> 8.97 us  [_show_ways(): lax.all_to_all(jnp.concatenate(in_order, 1), device_axis, 1, 1, tiled=True)]
  transfers between devices with their start and end apart: 5 -> 5, of which waited for: 5 -> 4; matrix products, arithmetic and copies ran while one was open for 30% -> 28% of each run, Pallas kernels for 0% -> 0%
where the time goes in v1:
time: 464 us; the launch traced here: 462 us
  waiting for transfers between devices  258 us (56%)
  local copies, waits for them, and re-layouts  75.1 us (16%)
  other arithmetic  54.7 us (12%)
  matrix products  44.5 us (10%)
  starting transfers between devices  15.2 us (3%)
  between operations  13.7 us (3%)
    all_to_all x1, waiting for transfers between devices, _show_ways(): lax.all_to_all(jnp.concatenate(in_order, 1), device_axis, 1, 1, tiled=True)  217 us
    all_to_all x2, local copies, waits for them, and re-layouts, _show_ways(): lax.all_to_all(jnp.concatenate(in_order, 1), device_axis, 1, 1, tiled=True)  43.2 us
    select_n x31, other arithmetic, turn(): jnp.where(position < mine, new, old)  38.3 us
    all_gather x2, waiting for transfers between devices, prefix(): pieces = jax.tree.map(lambda part: lax.all_gather(part, axis), value)  28.5 us
    unnamed x27, local copies, waits for them, and re-layouts  21.4 us
    dot_general x1, matrix products, per_device(): jnp.einsum('hqk,khd->qhd', near_p, value_rows, preferred_element_type=jnp...  14.3 us
    dot_general x1, matrix products, per_device(): jnp.dot(pieces, sections_change(out_weight), preferred_element_type=jnp.f...  13.8 us
    ppermute x2, waiting for transfers between devices, shifted(): return lax.ppermute(block, axis, route)  12.6 us
  transfers between devices with their start and end apart: 5, of which 4 were waited for; matrix products, arithmetic and copies ran while one was open for 28% of the time, Pallas kernels for 0%

profile of v1, /device:TPU:1, one launch (start us, length us, event | category | flops | bytes accessed | tf_op | source)
XLA Modules:
  0.0 462.1 jit_solution(2368963682081632369)
XLA Ops:
  6.5 2.0 convert_reduce_fusion.1
  8.6 0.7 copy-done.6
  9.3 2.0 convert_reduce_fusion
  11.4 0.7 copy-done.5
  12.1 2.9 copy.45
  15.2 0.1 constant_dynamic-update-slice_fusion.6
  16.2 5.7 %copy-done = bf16[2048,4096]{0,1:T(8,128)(2,1)} copy-done((bf16[2048,4096]{0,1:T(8,128)(2,1)}, bf16[2048,4096]{0,1:T(8,128)(2,1)S(1)}, u32[]{:S(2)}) %copy-start) | copy-done | bytes 16777240
  22.0 21.7 %copy.53 = bf16[2048,8,512]{2,0,1:T(8,128)(2,1)} copy(bf16[2048,8,512]{0,2,1:T(8,128)(2,1)} %bitcast.67) | data formatting | bytes 33554432 | tf_op jit(solution)/shard_map/all_to_all | solution.py:16
  43.6 9.0 %all-to-all-start = ((bf16[2048,8,512]{2,0,1:T(8,128)(2,1)}), bf16[2048,8,512]{2,0,1:T(8,128)(2,1)}, u32[]{:S(2)}, u32[]{:S(2)}) async-start(bf16[2048,8,512]{2,0,1:T(8,128)(2,1)} %copy.53), calls=%async_computation | async-start | bytes 33554432 | tf_op jit(solution)/shard_map/all_to_all | solution.py:16
  52.6 4.1 copy.36
  56.7 2.3 slice_bitcast_fusion
  59.0 4.1 collective-permute-start.1
  63.1 1.0 slice_bitcast_fusion.1
  64.2 2.1 collective-permute-start
  66.3 2.6 copy.35
  68.8 3.7 copy.58
  72.5 2.4 copy.39
  75.0 0.8 fusion.20
  75.8 2.2 collective-permute-done.1
  78.1 2.2 copy.38
  80.3 10.4 %collective-permute-done = bf16[256,2048]{1,0:T(8,128)(2,1)} collective-permute-done((bf16[256,2048]{1,0:T(8,128)(2,1)}, bf16[256,2048]{1,0:T(8,128)(2,1)}, u32[]{:S(2)}, u32[]{:S(2)}) %collective-permute-start) | collective-permute-done | bytes 1048608 | tf_op jit(solution)/shard_map/ppermute | solution.py:40
  90.7 2.3 copy.34
  93.0 12.2 %fusion.1 = (f32[16,512]{1,0:T(8,128)S(1)}, f32[16,768,512]{2,1,0:T(8,128)}) fusion(pred[512,768]{0,1:T(8,128)(4,1)S(1)} %fusion.20, bf16[512,16,128]{2,1,0:T(8,128)(2,1)S(1)} %bitcast.74, bf16[512,16,128]{2,0,1:T(8,128)(2,1)} %copy.39, bf16[256,16,128]{2,0,1:T(8,128)(2,1)} %copy.38), kind=kOutput, calls=%fused_computation.6 | convolution fusion | flops 1635770368 | bytes 30834688 | tf_op jit(solution)/shard_map/qhd,khd->hqk/dot_general | solution.py:98
  105.2 28.5 %all-gather.5.cloned.1.call-done = bf16[32,64,2048]{2,1,0:T(8,128)(2,1)} async-done(((bf16[1,64,2048]{2,1,0:T(8,128)(2,1)}), bf16[32,64,2048]{2,1,0:T(8,128)(2,1)}) %all-gather.5.cloned.1.call-update) | async-done | bytes 8388624 | tf_op jit(solution)/shard_map/all_gather | solution.py:25
  133.7 39.1 %while.16 = (s32[]{:T(128)}, bf16[64,2048]{1,0:T(8,128)(2,1)S(1)}, bf16[64,2048]{1,0:T(8,128)(2,1)S(1)}, s32[]{:T(128)}, bf16[32,64,2048]{2,1,0:T(8,128)(2,1)}, ...) while((s32[]{:T(128)}, bf16[64,2048]{1,0:T(8,128)(2,1)S(1)}, ...), condition=%wide.region_4.5_spmd.clone, body=%wide.region_3.4_spmd.clone.sunk | while | flops 786436 | bytes 1572973 | solution.py:34
  133.7 1.2 add_select_fusion.5
  135.0 1.2 add_select_fusion.5
  136.2 1.2 add_select_fusion.5
  137.5 1.2 add_select_fusion.5
  138.7 1.2 add_select_fusion.5
  140.0 1.2 add_select_fusion.5
  141.3 1.2 add_select_fusion.5
  142.5 1.2 add_select_fusion.5
  143.8 1.2 add_select_fusion.5
  145.0 1.2 add_select_fusion.5
  146.3 1.2 add_select_fusion.5
  147.6 1.2 add_select_fusion.5
  148.8 1.2 add_select_fusion.5
  150.1 1.2 add_select_fusion.5
  151.3 1.2 add_select_fusion.5
  152.6 1.2 add_select_fusion.5
  153.9 1.2 add_select_fusion.5
  155.1 1.2 add_select_fusion.5
  156.4 1.2 add_select_fusion.5
  157.6 1.2 add_select_fusion.5
  158.9 1.2 add_select_fusion.5
  160.2 1.2 add_select_fusion.5
  161.4 1.2 add_select_fusion.5
  162.7 1.2 add_select_fusion.5
  163.9 1.2 add_select_fusion.5
  165.2 1.2 add_select_fusion.5
  166.5 1.2 add_select_fusion.5
  167.7 1.2 add_select_fusion.5
  169.0 1.2 add_select_fusion.5
  170.3 1.2 add_select_fusion.5
  171.5 1.2 add_select_fusion.5
  172.8 1.5 fusion.42
  174.2 0.4 fusion.11
  174.6 11.1 %fusion = f32[16,512]{1,0:T(8,128)S(1)} fusion(f32[16,768,512]{2,1,0:T(8,128)} %get-tuple-element.153, f32[16,512]{1,0:T(8,128)S(1)} %max.7, pred[512,768]{0,1:T(8,128)(4,1)S(1)} %fusion.20), kind=kLoop, calls=%fused_computation.5 | loop fusion | flops 25157632 | bytes 25624576 | tf_op jit(solution)/shard_map/reduce_sum | solution.py:120
  185.8 2.8 fusion.21
  188.6 14.3 %add_convert_fusion = bf16[16,128,512]{2,1,0:T(8,128)(2,1)} fusion(f32[16,128,512]{2,1,0:T(8,128)} %fusion.21, f32[16,768,512]{2,1,0:T(8,128)} %get-tuple-element.153, f32[16,512]{1,0:T(8,128)S(1)} %add.130, f32[16,512]{1,0:T(8,128)S(1)} %max.7, pred[512,768]{0,1:T(8,128)(4,1)S(1)} %fusion.20, bf16[512,16,128]{0,2,1:T(8,128)(2,1)S(1)} %bitcast.73, ...), kind=kOutput, calls=%fused_computation.12 | convolution fusion | flops 1650458624 | bytes 35061760 | tf_op jit(solution)/shard_map/hqk,khd->qhd/dot_general | solution.py:123
  202.9 217.0 %all-to-all-done = bf16[2048,8,512]{2,0,1:T(8,128)(2,1)} async-done(((bf16[2048,8,512]{2,0,1:T(8,128)(2,1)}), bf16[2048,8,512]{2,0,1:T(8,128)(2,1)}, u32[]{:S(2)}, u32[]{:S(2)}) %all-to-all-start) | async-done | bytes 16777248 | tf_op jit(solution)/shard_map/all_to_all | solution.py:16
  419.8 21.6 %copy.54 = bf16[2048,8,512]{0,2,1:T(8,128)(2,1)} copy(bf16[2048,8,512]{2,0,1:T(8,128)(2,1)} %all-to-all-done) | data formatting | bytes 33554432 | tf_op jit(solution)/shard_map/all_to_all | solution.py:16
  441.4 13.8 %fusion.3 = bf16[1,512,4096]{2,1,0:T(8,128)(2,1)} fusion(bf16[512,2048]{0,1:T(8,128)(2,1)S(1)} %bitcast.77, bf16[2048,4096]{0,1:T(8,128)(2,1)} %bitcast.68), kind=kOutput, calls=%fused_computation.9 | convolution fusion | flops 8592031744 | bytes 23068672 | tf_op jit(solution)/shard_map/dot_general | solution.py:128
  (38 shorter events, 1.2 us)
Async XLA Ops:
  6.5 98.6 %all-gather.3.cloned.1.call-start = ((), (), s32[]{:S(2)}) async-start(), calls=%async_computation.1 | async-start | bytes 8650752 | tf_op jit(solution)/shard_map/all_gather | solution.py:25
  8.6 0.7 copy-start.6
  9.3 124.4 %all-gather.5.cloned.1.call-start = ((), (), s32[]{:S(2)}) async-start(), calls=%async_computation.2 | async-start | bytes 8650752 | tf_op jit(solution)/shard_map/all_gather | solution.py:25
  11.4 0.7 copy-start.5
  16.2 5.7 %copy-start = (bf16[2048,4096]{0,1:T(8,128)(2,1)}, bf16[2048,4096]{0,1:T(8,128)(2,1)S(1)}, u32[]{:S(2)}) copy-start(bf16[2048,4096]{0,1:T(8,128)(2,1)S(1)} %constant_dynamic-update-slice_fusion) | copy-start | bytes 50331652
  43.6 376.2 %all-to-all-start = ((bf16[2048,8,512]{2,0,1:T(8,128)(2,1)}), bf16[2048,8,512]{2,0,1:T(8,128)(2,1)}, u32[]{:S(2)}, u32[]{:S(2)}) async-start(bf16[2048,8,512]{2,0,1:T(8,128)(2,1)} %copy.53), calls=%async_computation | async-start | bytes 33554432 | tf_op jit(solution)/shard_map/all_to_all | solution.py:16
  52.6 10.5 %copy-start.1 = (bf16[1,512,2048]{2,1,0:T(8,128)(2,1)S(1)}, bf16[1,512,2048]{2,1,0:T(8,128)(2,1)}, u32[]{:S(2)}) copy-start(bf16[1,512,2048]{2,1,0:T(8,128)(2,1)} %param.8) | copy-start | bytes 6291460
  59.0 19.0 %collective-permute-start.1 = (bf16[256,2048]{0,1:T(8,128)(2,1)}, bf16[256,2048]{0,1:T(8,128)(2,1)}, u32[]{:S(2)}, u32[]{:S(2)}) collective-permute-start(bf16[256,2048]{0,1:T(8,128)(2,1)} %slice_bitcast_fusion), channel_id=1, source_target_pairs={{0,8},{8,16},{16,24},{24,32},{32,40},{40,48},{48,56},{56,64},{64,7... | collective-permute-start | bytes 3145736 | tf_op jit(solution)/shard_map/ppermute | solution.py:40
  64.2 26.5 %collective-permute-start = (bf16[256,2048]{1,0:T(8,128)(2,1)}, bf16[256,2048]{1,0:T(8,128)(2,1)}, u32[]{:S(2)}, u32[]{:S(2)}) collective-permute-start(bf16[256,2048]{1,0:T(8,128)(2,1)} %slice_bitcast_fusion.1), channel_id=1, source_target_pairs={{0,8},{8,16},{16,24},{24,32},{32,40},{40,48},{48,56},{56,64},{64,7... | collective-permute-start | bytes 3145736 | tf_op jit(solution)/shard_map/ppermute | solution.py:40
  68.8 3.7 copy-start.2
  74.9 18.1 %copy-start.4 = (bf16[64,8,16,128]{3,2,1,0:T(8,128)(2,1)S(1)}, bf16[64,8,16,128]{3,2,1,0:T(8,128)(2,1)}, u32[]{:S(2)}) copy-start(bf16[64,8,16,128]{3,2,1,0:T(8,128)(2,1)} %copy.58) | copy-start | bytes 6291460
  185.8 2.8 copy-start.3
  202.9 238.5 %copy-start.7 = (bf16[16,128,512]{2,1,0:T(8,128)(2,1)S(1)}, bf16[16,128,512]{2,1,0:T(8,128)(2,1)}, u32[]{:S(2)}) copy-start(bf16[16,128,512]{2,1,0:T(8,128)(2,1)} %add_convert_fusion) | copy-start | bytes 6291460
Sparse Core Ops, SparseCore 0:
  9.9 61.9 all-gather.2
  74.5 59.1 all-gather.4
